TPU v7x, 256 devices: a whole 4x4x8 slice. The times are simulated.
256 devices in a mesh: lon: 8 (over z), lat: 8 (over x, y_hi), dp: 4 (over y_lo, core).
Axes of the slice: x: 4, y: 4 (y_hi: 2, y_lo: 2; y = y_hi * 2 + y_lo), z: 8, core: 2. Of those that a mesh axis runs over, the one named last changes fastest.
Arguments:
- fields: bfloat16 [4, 256, 64, 1024], P('dp', None, 'lat', 'lon'), may hold values from -6 to 6
- weight_one: bfloat16 [9, 256, 256], replicated, may hold values from -0.125 to 0.125
- weight_two: bfloat16 [9, 256, 256], replicated, may hold values from -0.125 to 0.125
- edge_flips: int32 [7, 8], replicated, may hold values from 0 to 1, as said below
- cotangent: bfloat16 [4, 256, 64, 1024], P('dp', None, 'lat', 'lon'), may hold values from -6 to 6
Outputs:
- output: bfloat16 [4, 256, 64, 1024], P('dp', None, 'lat', 'lon')
- grad_fields: bfloat16 [4, 256, 64, 1024], P('dp', None, 'lat', 'lon')
- grad_one: float32 [9, 256, 256], replicated
- grad_two: float32 [9, 256, 256], replicated
Inputs may be any that keep to these rules, and one draw needn't show every extreme that they name: `edge_flips`: 0 on every edge inside a face; only row 8 // 2 - 1, the boundary between the band's two face rows, may hold 1, where the two faces meeting at that longitude tile store longitude in opposite orders.
All inputs are finite; a program needn't handle non-finite values.
Results may differ from a plain program's by a relative error of at most 0.0034.
Values may be sent and summed in bfloat16 or wider, within the bound.
No kernel may reach another device: no remote copies, remote signals or barrier semaphores. Data moves between devices by JAX's collectives and lax.ppermute only.
A program may use at most 128 MiB of HBM per device.

v0:
```python
import jax
import jax.numpy as jnp
from jax import lax
from jax.sharding import PartitionSpec as P


def with_halo(cells, sides, width, closed):
    for axis, dim in sides:
        count = lax.axis_size(axis)
        ends = count if closed else count - 1
        head = lax.slice_in_dim(cells, 0, width, axis=dim)
        tail = lax.slice_in_dim(cells, cells.shape[dim] - width, cells.shape[dim], axis=dim)
        cells = jnp.concatenate(
            [
                lax.ppermute(tail, axis, [(i, (i + 1) % count) for i in range(ends)]),
                cells,
                lax.ppermute(head, axis, [((i + 1) % count, i) for i in range(ends)]),
            ],
            axis=dim,
        )
    return cells


def oriented(line_cells, reverse_flag):
    return jnp.where(reverse_flag == 1, jnp.flip(line_cells, -1), line_cells)


def edge_flags(edge_flips):
    lat_index = lax.axis_index("lat")
    lon_index = lax.axis_index("lon")
    lat_count = lax.axis_size("lat")
    upper_flip = lax.dynamic_slice(edge_flips, (jnp.maximum(lat_index - 1, 0), lon_index), (1, 1))[
        0, 0
    ]
    lower_flip = lax.dynamic_slice(
        edge_flips, (jnp.minimum(lat_index, lat_count - 2), lon_index), (1, 1)
    )[0, 0]
    return (upper_flip, lower_flip, lat_index > 0, lat_index < lat_count - 1)


def padded(source, edge_info):
    upper_flip, lower_flip, has_upper, has_lower = edge_info
    extended = with_halo(source, (("lon", 3), ("lat", 2)), 1, True)
    top_rim = jnp.where(has_upper, extended[:, :, 0, :], jnp.zeros_like(extended[:, :, 0, :]))
    bottom = jnp.where(has_lower, extended[:, :, -1, :], jnp.zeros_like(extended[:, :, -1, :]))
    top_rim = oriented(top_rim, upper_flip)
    bottom = oriented(bottom, lower_flip)
    return jnp.concatenate(
        [top_rim[:, :, None, :], extended[:, :, 1:-1, :], bottom[:, :, None, :]], 2
    )


def patches_of(padded_in, tile_rows, tile_cols):
    return jnp.stack(
        [
            padded_in[:, :, tap_row : tap_row + tile_rows, tap_col : tap_col + tile_cols]
            for tap_row in range(3)
            for tap_col in range(3)
        ],
        1,
    )


def convolve(patches, weight):
    return jnp.einsum("toc,btchw->bohw", weight, patches, preferred_element_type=jnp.float32)


def transposed(grad_tile, weight, tile_rows, tile_cols):
    batch, chans = (grad_tile.shape[0], weight.shape[2])
    padded_grad = jnp.zeros((batch, chans, tile_rows + 2, tile_cols + 2), jnp.float32)
    for tap_row in range(3):
        for tap_col in range(3):
            tap_term = jnp.einsum(
                "oc,bohw->bchw",
                weight[3 * tap_row + tap_col],
                grad_tile,
                preferred_element_type=jnp.float32,
            )
            padded_grad = padded_grad.at[
                :, :, tap_row : tap_row + tile_rows, tap_col : tap_col + tile_cols
            ].add(tap_term)
    return padded_grad


def returned(padded_grad, edge_info):
    upper_flip, lower_flip, has_upper, has_lower = edge_info
    top_rim = oriented(padded_grad[:, :, 0, :], upper_flip)
    bottom = oriented(padded_grad[:, :, -1, :], lower_flip)
    rim_rows = jnp.stack([top_rim, bottom], 2)
    received = with_halo(rim_rows, (("lat", 2),), 1, False)
    interior = padded_grad[:, :, 1:-1, :]
    interior = interior.at[:, :, 0, :].add(received[:, :, 0, :])
    interior = interior.at[:, :, -1, :].add(received[:, :, -1, :])
    side_cols = jnp.stack([interior[..., 0], interior[..., -1]], -1)
    beside = with_halo(side_cols, (("lon", 3),), 1, True)
    result = interior[..., 1:-1]
    result = result.at[..., 0].add(beside[..., 0])
    result = result.at[..., -1].add(beside[..., -1])
    return result


def per_device(fields, weight_one, weight_two, edge_flips, cotangent):
    tile_rows, tile_cols = (fields.shape[2], fields.shape[3])
    edge_info = edge_flags(edge_flips)
    patch_in = patches_of(padded(fields, edge_info), tile_rows, tile_cols)
    hidden = convolve(patch_in, weight_one)
    activation = jax.nn.silu(hidden).astype(jnp.bfloat16)
    patch_act = patches_of(padded(activation, edge_info), tile_rows, tile_cols)
    output = (fields.astype(jnp.float32) + convolve(patch_act, weight_two)).astype(jnp.bfloat16)
    local_two = jnp.einsum(
        "bohw,btchw->toc", cotangent, patch_act, preferred_element_type=jnp.float32
    )
    back_act = returned(transposed(cotangent, weight_two, tile_rows, tile_cols), edge_info)
    sigmoid_h = jax.nn.sigmoid(hidden)
    back_hidden = (back_act * sigmoid_h * (1.0 + hidden * (1.0 - sigmoid_h))).astype(jnp.bfloat16)
    local_one = jnp.einsum(
        "bohw,btchw->toc", back_hidden, patch_in, preferred_element_type=jnp.float32
    )
    grad_one, grad_two = lax.psum((local_one, local_two), ("lon", "lat", "dp"))
    back_fields = returned(transposed(back_hidden, weight_one, tile_rows, tile_cols), edge_info)
    grad_fields = (cotangent.astype(jnp.float32) + back_fields).astype(jnp.bfloat16)
    return (output, grad_fields, grad_one, grad_two)


def solution(mesh):
    in_specs = (P("dp", None, "lat", "lon"), P(), P(), P(), P("dp", None, "lat", "lon"))
    out_specs = (P("dp", None, "lat", "lon"), P("dp", None, "lat", "lon"), P(), P())
    return jax.shard_map(
        per_device, mesh=mesh, in_specs=in_specs, out_specs=out_specs, check_vma=False
    )
```

profile of v0, /device:TPU:97, one launch (start us, length us, event | category | flops | bytes accessed | tf_op | source)
XLA Modules:
  0.0 453.6 jit_solution(17974031605681476931)
XLA Ops:
  8.6 2.9 collective-permute-start
  18.1 4.0 scatter-add.89
  22.1 3.2 add_select_fusion.1
  25.3 4.0 scatter-add.90
  51.2 5.2 %collective-permute-start.3 = (bf16[1,256,1,130]{1,3,2,0:T(8,128)(2,1)S(1)}, bf16[1,256,1,130]{1,3,2,0:T(8,128)(2,1)S(1)}, u32[]{:S(2)}, u32[]{:S(2)}) collective-permute-start(bf16[1,256,1,130]{1,3,2,0:T(8,128)(2,1)S(1)} %get-tuple-element.342), channel_id=1, source_target_pairs={{4,0},{8,4},{12,8},{16,12},{20,16},{24,20},{28,24},{0,28},{5,1},{9... | collective-permute-start | bytes 199688 | tf_op jit(solution)/shard_map/ppermute | solution.py:17
  57.8 5.5 %collective-permute-start.8 = (f32[1,256,1,130]{1,3,2,0:T(8,128)S(1)}, f32[1,256,1,130]{1,3,2,0:T(8,128)S(1)}, u32[]{:S(2)}, u32[]{:S(2)}) collective-permute-start(f32[1,256,1,130]{1,3,2,0:T(8,128)S(1)} %get-tuple-element.327), channel_id=1, source_target_pairs={{0,4},{4,8},{8,12},{12,16},{16,20},{20,24},{24,28},{1,5},{5,9},{9,... | collective-permute-start | bytes 399368 | tf_op jit(solution)/shard_map/ppermute | solution.py:15
  64.7 6.4 %collective-permute-done.2 = bf16[1,256,1,130]{1,3,2,0:T(8,128)(2,1)S(1)} collective-permute-done((bf16[1,256,1,130]{1,3,2,0:T(8,128)(2,1)S(1)}, bf16[1,256,1,130]{1,3,2,0:T(8,128)(2,1)S(1)}, u32[]{:S(2)}, u32[]{:S(2)}) %collective-permute-start.2) | collective-permute-done | bytes 66592 | tf_op jit(solution)/shard_map/ppermute | solution.py:15
  85.7 4.4 multiply_convert_fusion
  90.1 2.9 fusion.8
  97.6 7.2 %scatter-add.110 = f32[1,256,10,130]{1,3,2,0:T(8,128)S(1)} dynamic-update-slice(f32[1,256,10,130]{1,3,2,0:T(8,128)S(1)} %scatter-add.109, f32[1,256,8,128]{1,3,2,0:T(8,128)} %fusion.29, s32[]{:T(128)} %constant.657.clone.1, s32[]{:T(128)} %constant.657.clone.1, s32[]{:T(128)} %bitcast.51, s32[]{:T(128)} %bitcast.52) | dynamic-update-slice | bytes 2097156 | tf_op jit(solution)/shard_map/scatter-add | solution.py:81
  104.8 4.1 add_select_fusion
  108.9 7.2 %scatter-add.111 = f32[1,256,10,130]{1,3,2,0:T(8,128)S(1)} dynamic-update-slice(f32[1,256,10,130]{1,3,2,0:T(8,128)S(1)} %scatter-add.110, f32[1,256,8,128]{1,3,2,0:T(8,128)} %add_select_fusion, s32[]{:T(128)} %constant.657.clone.1, s32[]{:T(128)} %constant.657.clone.1, s32[]{:T(128)} %bitcast.57, s32[]{:T(128)} %bitcast.58) | dynamic-update-slice | bytes 2097156 | tf_op jit(solution)/shard_map/scatter-add | solution.py:81
  119.5 5.9 %scatter-add.115 = f32[1,256,10,130]{1,3,2,0:T(8,128)S(1)} dynamic-update-slice(f32[1,256,10,130]{1,3,2,0:T(8,128)S(1)} %fusion.31, f32[1,256,8,128]{1,3,2,0:T(8,128)} %fusion.32, s32[]{:T(128)} %constant.657.clone.1, s32[]{:T(128)} %constant.657.clone.1, s32[]{:T(128)} %constant.670.clone.1, s32[]{:T(128)} %constant.670.clone.1) | dynamic-update-slice | bytes 2097156 | tf_op jit(solution)/shard_map/scatter-add | solution.py:81
  127.6 5.9 %scatter-add.116 = f32[1,256,10,130]{1,3,2,0:T(8,128)S(1)} dynamic-update-slice(f32[1,256,10,130]{1,3,2,0:T(8,128)S(1)} %scatter-add.115, f32[1,256,8,128]{1,3,2,0:T(8,128)} %fusion.33, s32[]{:T(128)} %constant.657.clone.1, s32[]{:T(128)} %constant.657.clone.1, s32[]{:T(128)} %constant.670.clone.1, s32[]{:T(128)} %constant.667.clone.1) | dynamic-update-slice | bytes 2097156 | tf_op jit(solution)/shard_map/scatter-add | solution.py:81
  136.8 5.9 %scatter-add.120 = f32[1,256,10,130]{1,3,2,0:T(8,128)S(1)} dynamic-update-slice(f32[1,256,10,130]{1,3,2,0:T(8,128)S(1)} %fusion.35, f32[1,256,8,128]{1,3,2,0:T(8,128)} %fusion.36, s32[]{:T(128)} %constant.657.clone.1, s32[]{:T(128)} %constant.657.clone.1, s32[]{:T(128)} %constant.667.clone.1, s32[]{:T(128)} %constant.670.clone.1) | dynamic-update-slice | bytes 2097156 | tf_op jit(solution)/shard_map/scatter-add | solution.py:81
  145.6 5.9 %scatter-add.121 = f32[1,256,10,130]{1,3,2,0:T(8,128)S(1)} dynamic-update-slice(f32[1,256,10,130]{1,3,2,0:T(8,128)S(1)} %scatter-add.120, f32[1,256,8,128]{1,3,2,0:T(8,128)} %fusion.37, s32[]{:T(128)} %constant.657.clone.1, s32[]{:T(128)} %constant.657.clone.1, s32[]{:T(128)} %constant.667.clone.1, s32[]{:T(128)} %constant.667.clone.1) | dynamic-update-slice | bytes 2097156 | tf_op jit(solution)/shard_map/scatter-add | solution.py:81
  151.5 3.0 collective-permute-start.6
  162.9 2.9 fusion.11
  166.5 3.0 collective-permute-start.12
  171.4 6.0 %collective-permute-done.13 = f32[1,256,1,130]{1,3,2,0:T(8,128)S(1)} collective-permute-done((f32[1,256,1,130]{1,3,2,0:T(8,128)S(1)}, f32[1,256,1,130]{1,3,2,0:T(8,128)S(1)}, u32[]{:S(2)}, u32[]{:S(2)}) %collective-permute-start.13) | collective-permute-done | bytes 133152 | tf_op jit(solution)/shard_map/ppermute | solution.py:17
  180.2 3.8 fusion.41
  185.4 3.6 collective-permute-done.15
  190.3 251.3 %all-reduce.5.cloned.1.call-done = (f32[9,256,256]{1,2,0:T(8,128)}, f32[9,256,256]{1,2,0:T(8,128)}) async-done(((f32[9,256,256]{1,2,0:T(8,128)}, f32[9,256,256]{1,2,0:T(8,128)}), (f32[9,256,256]{1,2,0:T(8,128)}, f32[9,256,256]{1,2,0:T(8,128)})) %all-reduce.5.cloned.1.call-update) | async-done | bytes 4718608 | tf_op jit(solution)/shard_map/psum | solution.py:119
  441.6 3.2 copy.38
  (144 shorter events, 80.1 us)
Async XLA Ops:
  7.2 7.0 %copy-start = (bf16[1,256,8,128]{3,2,1,0:T(8,128)(2,1)S(1)}, bf16[1,256,8,128]{3,2,1,0:T(8,128)(2,1)}, u32[]{:S(2)}) copy-start(bf16[1,256,8,128]{3,2,1,0:T(8,128)(2,1)} %param.61) | copy-start | bytes 1572868
  7.2 434.4 %all-reduce.5.cloned.1.call-start = ((), (), s32[]{:S(2)}) async-start(), calls=%async_computation | async-start | bytes 9437184 | tf_op jit(solution)/shard_map/psum | solution.py:119
  8.6 42.5 %collective-permute-start = (bf16[1,256,8,1]{1,3,2,0:T(2,128)(2,1)S(1)}, bf16[1,256,8,1]{1,3,2,0:T(2,128)(2,1)S(1)}, u32[]{:S(2)}, u32[]{:S(2)}) collective-permute-start(bf16[1,256,8,1]{1,3,2,0:T(2,128)(2,1)S(1)} %get-tuple-element.346), channel_id=1, source_target_pairs={{0,32},{32,64},{64,96},{96,128},{128,160},{160,192},{192,224},{224... | collective-permute-start | bytes 12296 | tf_op jit(solution)/shard_map/ppermute | solution.py:15
  11.5 39.6 %collective-permute-start.1 = (bf16[1,256,8,1]{1,3,2,0:T(2,128)(2,1)S(1)}, bf16[1,256,8,1]{1,3,2,0:T(2,128)(2,1)S(1)}, u32[]{:S(2)}, u32[]{:S(2)}) collective-permute-start(bf16[1,256,8,1]{1,3,2,0:T(2,128)(2,1)S(1)} %get-tuple-element.347), channel_id=1, source_target_pairs={{32,0},{64,32},{96,64},{128,96},{160,128},{192,160},{224,192},{0,2... | collective-permute-start | bytes 12296 | tf_op jit(solution)/shard_map/ppermute | solution.py:17
  51.2 13.1 %collective-permute-start.3 = (bf16[1,256,1,130]{1,3,2,0:T(8,128)(2,1)S(1)}, bf16[1,256,1,130]{1,3,2,0:T(8,128)(2,1)S(1)}, u32[]{:S(2)}, u32[]{:S(2)}) collective-permute-start(bf16[1,256,1,130]{1,3,2,0:T(8,128)(2,1)S(1)} %get-tuple-element.342), channel_id=1, source_target_pairs={{4,0},{8,4},{12,8},{16,12},{20,16},{24,20},{28,24},{0,28},{5,1},{9... | collective-permute-start | bytes 199688 | tf_op jit(solution)/shard_map/ppermute | solution.py:17
  56.5 17.0 %collective-permute-start.9 = (f32[1,256,1,130]{1,3,2,0:T(8,128)S(1)}, f32[1,256,1,130]{1,3,2,0:T(8,128)S(1)}, u32[]{:S(2)}, u32[]{:S(2)}) collective-permute-start(f32[1,256,1,130]{1,3,2,0:T(8,128)S(1)} %get-tuple-element.326), channel_id=1, source_target_pairs={{4,0},{8,4},{12,8},{16,12},{20,16},{24,20},{28,24},{5,1},{9,5},{13... | collective-permute-start | bytes 399368 | tf_op jit(solution)/shard_map/ppermute | solution.py:17
  57.8 14.8 %collective-permute-start.8 = (f32[1,256,1,130]{1,3,2,0:T(8,128)S(1)}, f32[1,256,1,130]{1,3,2,0:T(8,128)S(1)}, u32[]{:S(2)}, u32[]{:S(2)}) collective-permute-start(f32[1,256,1,130]{1,3,2,0:T(8,128)S(1)} %get-tuple-element.327), channel_id=1, source_target_pairs={{0,4},{4,8},{8,12},{12,16},{16,20},{20,24},{24,28},{1,5},{5,9},{9,... | collective-permute-start | bytes 399368 | tf_op jit(solution)/shard_map/ppermute | solution.py:15
  64.3 6.8 %collective-permute-start.2 = (bf16[1,256,1,130]{1,3,2,0:T(8,128)(2,1)S(1)}, bf16[1,256,1,130]{1,3,2,0:T(8,128)(2,1)S(1)}, u32[]{:S(2)}, u32[]{:S(2)}) collective-permute-start(bf16[1,256,1,130]{1,3,2,0:T(8,128)(2,1)S(1)} %get-tuple-element.343), channel_id=1, source_target_pairs={{0,4},{4,8},{8,12},{12,16},{16,20},{20,24},{24,28},{28,0},{1,5},{5... | collective-permute-start | bytes 199688 | tf_op jit(solution)/shard_map/ppermute | solution.py:15
  73.6 12.2 %copy-start.5 = (bf16[9,256,256]{2,1,0:T(8,128)(2,1)S(1)}, bf16[9,256,256]{2,1,0:T(8,128)(2,1)}, u32[]{:S(2)}) copy-start(bf16[9,256,256]{2,1,0:T(8,128)(2,1)} %param.58) | copy-start | bytes 3538948
  73.6 6.1 %collective-permute-start.10 = (f32[1,256,8,1]{1,3,2,0:T(1,128)S(1)}, f32[1,256,8,1]{1,3,2,0:T(1,128)S(1)}, u32[]{:S(2)}, u32[]{:S(2)}) collective-permute-start(f32[1,256,8,1]{1,3,2,0:T(1,128)S(1)} %get-tuple-element.333), channel_id=1, source_target_pairs={{0,32},{32,64},{64,96},{96,128},{128,160},{160,192},{192,224},{224... | collective-permute-start | bytes 24584 | tf_op jit(solution)/shard_map/ppermute | solution.py:15
  79.7 3.7 collective-permute-start.11
  85.7 4.4 copy-start.9
  96.0 46.7 %collective-permute-start.4 = (bf16[1,256,8,1]{1,3,2,0:T(2,128)(2,1)S(1)}, bf16[1,256,8,1]{1,3,2,0:T(2,128)(2,1)S(1)}, u32[]{:S(2)}, u32[]{:S(2)}) collective-permute-start(bf16[1,256,8,1]{1,3,2,0:T(2,128)(2,1)S(1)} %get-tuple-element.344), channel_id=1, source_target_pairs={{0,32},{32,64},{64,96},{96,128},{128,160},{160,192},{192,224},{224... | collective-permute-start | bytes 12296 | tf_op jit(solution)/shard_map/ppermute | solution.py:15
  96.6 46.1 %collective-permute-start.5 = (bf16[1,256,8,1]{1,3,2,0:T(2,128)(2,1)S(1)}, bf16[1,256,8,1]{1,3,2,0:T(2,128)(2,1)S(1)}, u32[]{:S(2)}, u32[]{:S(2)}) collective-permute-start(bf16[1,256,8,1]{1,3,2,0:T(2,128)(2,1)S(1)} %get-tuple-element.345), channel_id=1, source_target_pairs={{32,0},{64,32},{96,64},{128,96},{160,128},{192,160},{224,192},{0,2... | collective-permute-start | bytes 12296 | tf_op jit(solution)/shard_map/ppermute | solution.py:17
  143.4 11.1 %collective-permute-start.7 = (bf16[1,256,1,130]{1,3,2,0:T(8,128)(2,1)}, bf16[1,256,1,130]{1,3,2,0:T(8,128)(2,1)}, u32[]{:S(2)}, u32[]{:S(2)}) collective-permute-start(bf16[1,256,1,130]{1,3,2,0:T(8,128)(2,1)} %get-tuple-element.338), channel_id=1, source_target_pairs={{4,0},{8,4},{12,8},{16,12},{20,16},{24,20},{28,24},{0,28},{5,1},{9... | collective-permute-start | bytes 199688 | tf_op jit(solution)/shard_map/ppermute | solution.py:17
  145.6 5.9 %copy-start.7 = (bf16[1,256,1,130]{1,3,2,0:T(8,128)(2,1)S(1)}, bf16[1,256,1,130]{1,3,2,0:T(8,128)(2,1)}, u32[]{:S(2)}) copy-start(bf16[1,256,1,130]{1,3,2,0:T(8,128)(2,1)} %get-tuple-element.339) | copy-start | bytes 199684
  151.5 6.9 %collective-permute-start.6 = (bf16[1,256,1,130]{1,3,2,0:T(8,128)(2,1)S(1)}, bf16[1,256,1,130]{1,3,2,0:T(8,128)(2,1)S(1)}, u32[]{:S(2)}, u32[]{:S(2)}) collective-permute-start(bf16[1,256,1,130]{1,3,2,0:T(8,128)(2,1)S(1)} %copy-done.7), channel_id=1, source_target_pairs={{0,4},{4,8},{8,12},{12,16},{16,20},{20,24},{24,28},{28,0},{1,5},{5... | collective-permute-start | bytes 199688 | tf_op jit(solution)/shard_map/ppermute | solution.py:15
  166.5 4.9 %collective-permute-start.12 = (f32[1,256,1,130]{1,3,2,0:T(8,128)S(1)}, f32[1,256,1,130]{1,3,2,0:T(8,128)S(1)}, u32[]{:S(2)}, u32[]{:S(2)}) collective-permute-start(f32[1,256,1,130]{1,3,2,0:T(8,128)S(1)} %get-tuple-element.323), channel_id=1, source_target_pairs={{0,4},{4,8},{8,12},{12,16},{16,20},{20,24},{24,28},{1,5},{5,9},{9,... | collective-permute-start | bytes 399368 | tf_op jit(solution)/shard_map/ppermute | solution.py:15
  169.8 10.4 %copy-start.6 = (bf16[9,256,256]{2,1,0:T(8,128)(2,1)S(1)}, bf16[9,256,256]{2,1,0:T(8,128)(2,1)}, u32[]{:S(2)}) copy-start(bf16[9,256,256]{2,1,0:T(8,128)(2,1)} %param.59) | copy-start | bytes 3538948
  169.9 7.4 %collective-permute-start.13 = (f32[1,256,1,130]{1,3,2,0:T(8,128)S(1)}, f32[1,256,1,130]{1,3,2,0:T(8,128)S(1)}, u32[]{:S(2)}, u32[]{:S(2)}) collective-permute-start(f32[1,256,1,130]{1,3,2,0:T(8,128)S(1)} %get-tuple-element.322), channel_id=1, source_target_pairs={{4,0},{8,4},{12,8},{16,12},{20,16},{24,20},{28,24},{5,1},{9,5},{13... | collective-permute-start | bytes 399368 | tf_op jit(solution)/shard_map/ppermute | solution.py:17
  178.4 6.9 %collective-permute-start.14 = (f32[1,256,8,1]{1,3,2,0:T(1,128)S(1)}, f32[1,256,8,1]{1,3,2,0:T(1,128)S(1)}, u32[]{:S(2)}, u32[]{:S(2)}) collective-permute-start(f32[1,256,8,1]{1,3,2,0:T(1,128)S(1)} %get-tuple-element.331), channel_id=1, source_target_pairs={{0,32},{32,64},{64,96},{96,128},{128,160},{160,192},{192,224},{224... | collective-permute-start | bytes 24584 | tf_op jit(solution)/shard_map/ppermute | solution.py:15
  180.2 4.9 %copy-start.3 = (f32[1,256,8,130]{1,3,2,0:T(8,128)S(1)}, f32[1,256,8,130]{1,3,2,0:T(8,128)}, u32[]{:S(2)}) copy-start(f32[1,256,8,130]{1,3,2,0:T(8,128)} %copy-done.2) | copy-start | bytes 3194884
  185.2 3.8 collective-permute-start.15
  441.6 3.2 copy-start.4
  (4 other events, 6.5 us)
Sparse Core Ops, SparseCore 0:
  165.9 275.6 all-reduce.4
where the time goes:
time: 455 us; the launch traced here: 454 us
  waiting for transfers between devices  272 us (60%)
  local copies, waits for them, and re-layouts  84.1 us (18%)
  matrix products  46.6 us (10%)
  starting transfers between devices  28.6 us (6%)
  between operations  16.1 us (4%)
  other arithmetic  6.15 us (1%)
    psum x1, waiting for transfers between devices, per_device(): grad_one, grad_two = lax.psum((local_one, local_two), ('lon', 'lat', 'dp'))  251 us
    scatter-add x14, local copies, waits for them, and re-layouts, transposed(): padded_grad = padded_grad.at[:, :, tap_row:tap_row + tile_rows, tap_col:t...  57 us
    dot_general x18, matrix products, transposed(): jnp.einsum('oc,bohw->bchw', weight[3 * tap_row + tap_col], grad_tile, pre...  32.6 us
    ppermute x8, starting transfers between devices, with_halo(): lax.ppermute(tail, axis, [(i, (i + 1) % count) for i in range(ends)])  19.6 us
    unnamed x40, local copies, waits for them, and re-layouts  16.1 us
    ppermute x8, waiting for transfers between devices, with_halo(): lax.ppermute(head, axis, [((i + 1) % count, i) for i in range(ends)])  11.8 us
  transfers between devices with their start and end apart: 17, of which 6 were waited for; matrix products, arithmetic and copies ran while one was open for 23% of the time, Pallas kernels for 0%

commit v1 on v0

--- a/solution.py
+++ b/solution.py
@@ -116,7 +116,9 @@
     local_one = jnp.einsum(
         "bohw,btchw->toc", back_hidden, patch_in, preferred_element_type=jnp.float32
     )
-    grad_one, grad_two = lax.psum((local_one, local_two), ("lon", "lat", "dp"))
+    grad_one, grad_two = lax.psum(
+        lax.psum((local_one, local_two), axis_name=("lat", "dp")), axis_name="lon"
+    )
     back_fields = returned(transposed(back_hidden, weight_one, tile_rows, tile_cols), edge_info)
     grad_fields = (cotangent.astype(jnp.float32) + back_fields).astype(jnp.bfloat16)
     return (output, grad_fields, grad_one, grad_two)

time: 455 us -> 379 us (0.83)
  waiting for transfers between devices: 272 us -> 180 us
  other arithmetic: 6.15 us -> 11.4 us
    psum x1 -> x2, waiting for transfers between devices: 251 us -> 155 us  [the longest x1 120 us: per_device(): lax.psum((local_one, local_two), axis_name=('lat', 'dp'))]
    rev x8, local copies, waits for them, and re-layouts: 2.56 us -> 7.26 us  [oriented(): return jnp.where(reverse_flag == 1, jnp.flip(line_cells, -1), line_cells)]
    unnamed x40 -> x44, local copies, waits for them, and re-layouts: 16.1 us -> 16.6 us
  transfers between devices with their start and end apart: 17 -> 18, of which waited for: 6 -> 10; matrix products, arithmetic and copies ran while one was open for 23% -> 32% of each run, Pallas kernels for 0% -> 0%
where the time goes in v1:
time: 379 us; the launch traced here: 375 us
  waiting for transfers between devices  180 us (47%)
  local copies, waits for them, and re-layouts  87.7 us (23%)
  matrix products  48.9 us (13%)
  starting transfers between devices  31.2 us (8%)
  between operations  16.1 us (4%)
  other arithmetic  11.4 us (3%)
    psum x1, waiting for transfers between devices, per_device(): lax.psum((local_one, local_two), axis_name=('lat', 'dp'))  120 us
    scatter-add x14, local copies, waits for them, and re-layouts, transposed(): padded_grad = padded_grad.at[:, :, tap_row:tap_row + tile_rows, tap_col:t...  56.5 us
    psum x1, waiting for transfers between devices, per_device(): lax.psum(lax.psum((local_one, local_two), axis_name=('lat', 'dp')), axis_...  35.3 us
    dot_general x18, matrix products, transposed(): jnp.einsum('oc,bohw->bchw', weight[3 * tap_row + tap_col], grad_tile, pre...  34.4 us
    ppermute x8, starting transfers between devices, with_halo(): lax.ppermute(tail, axis, [(i, (i + 1) % count) for i in range(ends)])  20 us
    unnamed x44, local copies, waits for them, and re-layouts  16.6 us
    ppermute x8, waiting for transfers between devices, with_halo(): lax.ppermute(head, axis, [((i + 1) % count, i) for i in range(ends)])  14 us
    ppermute x8, starting transfers between devices, with_halo(): lax.ppermute(head, axis, [((i + 1) % count, i) for i in range(ends)])  11.2 us
  transfers between devices with their start and end apart: 18, of which 10 were waited for; matrix products, arithmetic and copies ran while one was open for 32% of the time, Pallas kernels for 0%

profile of v1, /device:TPU:97, one launch (start us, length us, event | category | flops | bytes accessed | tf_op | source)
XLA Modules:
  0.0 375.1 jit_solution(8747877026842868022)
XLA Ops:
  8.6 2.9 collective-permute-start
  17.9 3.8 %scatter-add.89 = f32[1,256,10,130]{1,3,2,0:T(8,128)S(1)} dynamic-update-slice(f32[1,256,10,130]{1,3,2,0:T(8,128)S(1)} %scatter-add.86, f32[1,256,8,128]{1,3,2,0:T(8,128)S(1)} %fusion.20, s32[]{:T(128)} %constant.657.clone.1, s32[]{:T(128)} %constant.657.clone.1, s32[]{:T(128)} %bitcast.51, s32[]{:T(128)} %bitcast.52) | dynamic-update-slice | bytes 2097156 | tf_op jit(solution)/shard_map/scatter-add | solution.py:81
  21.7 3.1 add_select_fusion.1
  24.8 4.0 %scatter-add.90 = f32[1,256,10,130]{1,3,2,0:T(8,128)S(1)} dynamic-update-slice(f32[1,256,10,130]{1,3,2,0:T(8,128)S(1)} %scatter-add.89, f32[1,256,8,128]{1,3,2,0:T(8,128)S(1)} %add_select_fusion.1, s32[]{:T(128)} %constant.657.clone.1, s32[]{:T(128)} %constant.657.clone.1, s32[]{:T(128)} %bitcast.57, s32[]{:T(128)} %bitcast.58) | dynamic-update-slice | bytes 2097156 | tf_op jit(solution)/shard_map/scatter-add | solution.py:81
  51.3 5.1 %collective-permute-start.3 = (bf16[1,256,1,130]{1,3,2,0:T(8,128)(2,1)}, bf16[1,256,1,130]{1,3,2,0:T(8,128)(2,1)}, u32[]{:S(2)}, u32[]{:S(2)}) collective-permute-start(bf16[1,256,1,130]{1,3,2,0:T(8,128)(2,1)} %get-tuple-element.344), channel_id=1, source_target_pairs={{4,0},{8,4},{12,8},{16,12},{20,16},{24,20},{28,24},{0,28},{5,1},{9... | collective-permute-start | bytes 199688 | tf_op jit(solution)/shard_map/ppermute | solution.py:17
  58.5 6.2 %collective-permute-start.8 = (f32[1,256,1,130]{1,3,2,0:T(8,128)}, f32[1,256,1,130]{1,3,2,0:T(8,128)}, u32[]{:S(2)}, u32[]{:S(2)}) collective-permute-start(f32[1,256,1,130]{1,3,2,0:T(8,128)} %get-tuple-element.329), channel_id=1, source_target_pairs={{0,4},{4,8},{8,12},{12,16},{16,20},{20,24},{24,28},{1,5},{5,9},{9,... | collective-permute-start | bytes 399368 | tf_op jit(solution)/shard_map/ppermute | solution.py:15
  92.5 4.7 %multiply_convert_fusion = (bf16[1,256,8,128]{1,3,2,0:T(8,128)(2,1)S(1)}, bf16[1,256,8,128]{1,3,2,0:T(8,128)(2,1)S(1)}) fusion(f32[1,256,8,128]{1,3,2,0:T(8,128)} %scatter-add.106, bf16[9,256,256]{2,1,0:T(8,128)(2,1)} %param.58, bf16[1,9,256,8,128]{2,4,1,3,0:T(8,128)(2,1)} %copy-done.10), kind=kOutput, calls=%fused_computation.55 | convolution fusion | flops 1210843136 | bytes 7995392 | tf_op jit(solution)/shard_map/toc,btchw->bohw/dot_general | solution.py:65
  103.8 2.9 fusion.8
  107.8 5.6 %collective-permute-done.6 = bf16[1,256,1,130]{1,3,2,0:T(8,128)(2,1)S(1)} collective-permute-done((bf16[1,256,1,130]{1,3,2,0:T(8,128)(2,1)S(1)}, bf16[1,256,1,130]{1,3,2,0:T(8,128)(2,1)S(1)}, u32[]{:S(2)}, u32[]{:S(2)}) %collective-permute-start.6) | collective-permute-done | bytes 66592 | tf_op jit(solution)/shard_map/ppermute | solution.py:15
  122.4 120.1 %all-reduce.7.cloned.1.call-done = (f32[9,256,256]{1,2,0:T(8,128)}, f32[9,256,256]{1,2,0:T(8,128)}) async-done(((f32[9,256,256]{1,2,0:T(8,128)}, f32[9,256,256]{1,2,0:T(8,128)}), (f32[9,256,256]{1,2,0:T(8,128)}, f32[9,256,256]{1,2,0:T(8,128)})) %all-reduce.7.cloned.1.call-update) | async-done | bytes 4718608 | tf_op jit(solution)/shard_map/psum | solution.py:120
  242.6 3.7 fusion.29
  246.3 7.0 %scatter-add.110 = f32[1,256,10,130]{1,3,2,0:T(8,128)S(1)} dynamic-update-slice(f32[1,256,10,130]{1,3,2,0:T(8,128)S(1)} %scatter-add.109, f32[1,256,8,128]{1,3,2,0:T(8,128)} %fusion.29, s32[]{:T(128)} %constant.657.clone.1, s32[]{:T(128)} %constant.657.clone.1, s32[]{:T(128)} %bitcast.51, s32[]{:T(128)} %bitcast.52) | dynamic-update-slice | bytes 2097156 | tf_op jit(solution)/shard_map/scatter-add | solution.py:81
  253.3 4.1 %add_select_fusion = f32[1,256,8,128]{1,3,2,0:T(8,128)} fusion(f32[1,256,10,130]{1,3,2,0:T(8,128)S(1)} %scatter-add.110, s32[]{:T(128)} %bitcast.57, s32[]{:T(128)} %bitcast.58, bf16[1,256,8,128]{1,3,2,0:T(8,128)(2,1)S(1)} %get-tuple-element.336, pred[]{:T(512)} %and_reduce_fusion, bf16[9,256,256]{2,1,0:T(8,128)(2,1)} %param.58), kind=kOutput, calls=%fused_computation.10 | convolution fusion | flops 134742016 | bytes 2754048 | tf_op jit(solution)/shard_map/oc,bohw->bchw/dot_general | solution.py:73
  257.4 7.2 %scatter-add.111 = f32[1,256,10,130]{1,3,2,0:T(8,128)S(1)} dynamic-update-slice(f32[1,256,10,130]{1,3,2,0:T(8,128)S(1)} %scatter-add.110, f32[1,256,8,128]{1,3,2,0:T(8,128)} %add_select_fusion, s32[]{:T(128)} %constant.657.clone.1, s32[]{:T(128)} %constant.657.clone.1, s32[]{:T(128)} %bitcast.57, s32[]{:T(128)} %bitcast.58) | dynamic-update-slice | bytes 2097156 | tf_op jit(solution)/shard_map/scatter-add | solution.py:81
  268.0 5.9 %scatter-add.115 = f32[1,256,10,130]{1,3,2,0:T(8,128)S(1)} dynamic-update-slice(f32[1,256,10,130]{1,3,2,0:T(8,128)S(1)} %fusion.31, f32[1,256,8,128]{1,3,2,0:T(8,128)} %fusion.32, s32[]{:T(128)} %constant.657.clone.1, s32[]{:T(128)} %constant.657.clone.1, s32[]{:T(128)} %constant.670.clone.1, s32[]{:T(128)} %constant.670.clone.1) | dynamic-update-slice | bytes 2097156 | tf_op jit(solution)/shard_map/scatter-add | solution.py:81
  276.0 5.9 %scatter-add.116 = f32[1,256,10,130]{1,3,2,0:T(8,128)S(1)} dynamic-update-slice(f32[1,256,10,130]{1,3,2,0:T(8,128)S(1)} %scatter-add.115, f32[1,256,8,128]{1,3,2,0:T(8,128)} %fusion.33, s32[]{:T(128)} %constant.657.clone.1, s32[]{:T(128)} %constant.657.clone.1, s32[]{:T(128)} %constant.670.clone.1, s32[]{:T(128)} %constant.667.clone.1) | dynamic-update-slice | bytes 2097156 | tf_op jit(solution)/shard_map/scatter-add | solution.py:81
  285.3 5.9 %scatter-add.120 = f32[1,256,10,130]{1,3,2,0:T(8,128)S(1)} dynamic-update-slice(f32[1,256,10,130]{1,3,2,0:T(8,128)S(1)} %fusion.35, f32[1,256,8,128]{1,3,2,0:T(8,128)} %fusion.36, s32[]{:T(128)} %constant.657.clone.1, s32[]{:T(128)} %constant.657.clone.1, s32[]{:T(128)} %constant.667.clone.1, s32[]{:T(128)} %constant.670.clone.1) | dynamic-update-slice | bytes 2097156 | tf_op jit(solution)/shard_map/scatter-add | solution.py:81
  293.3 5.9 %scatter-add.121 = f32[1,256,10,130]{1,3,2,0:T(8,128)S(1)} dynamic-update-slice(f32[1,256,10,130]{1,3,2,0:T(8,128)S(1)} %scatter-add.120, f32[1,256,8,128]{1,3,2,0:T(8,128)} %fusion.37, s32[]{:T(128)} %constant.657.clone.1, s32[]{:T(128)} %constant.657.clone.1, s32[]{:T(128)} %constant.667.clone.1, s32[]{:T(128)} %constant.667.clone.1) | dynamic-update-slice | bytes 2097156 | tf_op jit(solution)/shard_map/scatter-add | solution.py:81
  300.5 4.3 %collective-permute-start.12 = (f32[1,256,1,130]{1,3,2,0:T(8,128)}, f32[1,256,1,130]{1,3,2,0:T(8,128)S(1)}, u32[]{:S(2)}, u32[]{:S(2)}) collective-permute-start(f32[1,256,1,130]{1,3,2,0:T(8,128)} %get-tuple-element.325), channel_id=1, source_target_pairs={{0,4},{4,8},{8,12},{12,16},{16,20},{20,24},{24,28},{1,5},{5,9},{9,... | collective-permute-start | bytes 399368 | tf_op jit(solution)/shard_map/ppermute | solution.py:15
  307.5 5.8 %collective-permute-done.13 = f32[1,256,1,130]{1,3,2,0:T(8,128)S(1)} collective-permute-done((f32[1,256,1,130]{1,3,2,0:T(8,128)S(1)}, f32[1,256,1,130]{1,3,2,0:T(8,128)S(1)}, u32[]{:S(2)}, u32[]{:S(2)}) %collective-permute-start.13) | collective-permute-done | bytes 133152 | tf_op jit(solution)/shard_map/ppermute | solution.py:17
  316.8 4.0 %fusion.41 = bf16[1,256,8,128]{1,3,2,0:T(8,128)(2,1)S(1)} fusion(bf16[1,9,256,8,128]{2,4,3,1,0:T(8,128)(2,1)} %copy-done.12, bf16[9,256,256]{2,1,0:T(8,128)(2,1)S(1)} %copy-done.5, bf16[1,256,8,128]{1,3,2,0:T(8,128)(2,1)S(1)} %copy.9), kind=kOutput, calls=%fused_computation.51 | convolution fusion | flops 1208745984 | bytes 6946816 | tf_op jit(solution)/shard_map/toc,btchw->bohw/dot_general | solution.py:65
  322.2 4.3 %collective-permute-done.15 = f32[1,256,8,1]{1,3,2,0:T(1,128)S(1)} collective-permute-done((f32[1,256,8,1]{1,3,2,0:T(1,128)S(1)}, f32[1,256,8,1]{1,3,2,0:T(1,128)S(1)}, u32[]{:S(2)}, u32[]{:S(2)}) %collective-permute-start.15) | collective-permute-done | bytes 8224 | tf_op jit(solution)/shard_map/ppermute | solution.py:17
  327.8 35.3 %all-reduce.9.cloned.1.call-done = (f32[9,256,256]{1,2,0:T(8,128)}, f32[9,256,256]{1,2,0:T(8,128)}) async-done(((f32[9,256,256]{1,2,0:T(8,128)}, f32[9,256,256]{1,2,0:T(8,128)}), (f32[9,256,256]{1,2,0:T(8,128)}, f32[9,256,256]{1,2,0:T(8,128)})) %all-reduce.9.cloned.1.call-update) | async-done | bytes 4718608 | tf_op jit(solution)/shard_map/psum | solution.py:119
  363.1 3.2 copy.38
  (151 shorter events, 98.3 us)
Async XLA Ops:
  7.2 6.9 %copy-start = (bf16[1,256,8,128]{3,2,1,0:T(8,128)(2,1)S(1)}, bf16[1,256,8,128]{3,2,1,0:T(8,128)(2,1)}, u32[]{:S(2)}) copy-start(bf16[1,256,8,128]{3,2,1,0:T(8,128)(2,1)} %param.61) | copy-start | bytes 1572868
  7.2 235.4 %all-reduce.7.cloned.1.call-start = ((), (), s32[]{:S(2)}) async-start(), calls=%async_computation | async-start | bytes 9437184 | tf_op jit(solution)/shard_map/psum | solution.py:120
  8.6 42.0 %collective-permute-start = (bf16[1,256,8,1]{1,3,2,0:T(2,128)(2,1)S(1)}, bf16[1,256,8,1]{1,3,2,0:T(2,128)(2,1)S(1)}, u32[]{:S(2)}, u32[]{:S(2)}) collective-permute-start(bf16[1,256,8,1]{1,3,2,0:T(2,128)(2,1)S(1)} %get-tuple-element.348), channel_id=1, source_target_pairs={{0,32},{32,64},{64,96},{96,128},{128,160},{160,192},{192,224},{224... | collective-permute-start | bytes 12296 | tf_op jit(solution)/shard_map/ppermute | solution.py:15
  11.5 39.1 %collective-permute-start.1 = (bf16[1,256,8,1]{1,3,2,0:T(2,128)(2,1)S(1)}, bf16[1,256,8,1]{1,3,2,0:T(2,128)(2,1)S(1)}, u32[]{:S(2)}, u32[]{:S(2)}) collective-permute-start(bf16[1,256,8,1]{1,3,2,0:T(2,128)(2,1)S(1)} %get-tuple-element.349), channel_id=1, source_target_pairs={{32,0},{64,32},{96,64},{128,96},{160,128},{192,160},{224,192},{0,2... | collective-permute-start | bytes 12296 | tf_op jit(solution)/shard_map/ppermute | solution.py:17
  50.6 14.0 %copy-start.6 = (bf16[1,256,8,1]{1,3,2,0:T(2,128)(2,1)}, bf16[1,256,8,1]{1,3,2,0:T(2,128)(2,1)S(1)}, u32[]{:S(2)}) copy-start(bf16[1,256,8,1]{1,3,2,0:T(2,128)(2,1)S(1)} %collective-permute-done) | copy-start | bytes 12292
  50.6 14.0 %copy-start.8 = (bf16[1,256,8,1]{1,3,2,0:T(2,128)(2,1)}, bf16[1,256,8,1]{1,3,2,0:T(2,128)(2,1)S(1)}, u32[]{:S(2)}) copy-start(bf16[1,256,8,1]{1,3,2,0:T(2,128)(2,1)S(1)} %collective-permute-done.1) | copy-start | bytes 12292
  51.3 13.5 %collective-permute-start.3 = (bf16[1,256,1,130]{1,3,2,0:T(8,128)(2,1)}, bf16[1,256,1,130]{1,3,2,0:T(8,128)(2,1)}, u32[]{:S(2)}, u32[]{:S(2)}) collective-permute-start(bf16[1,256,1,130]{1,3,2,0:T(8,128)(2,1)} %get-tuple-element.344), channel_id=1, source_target_pairs={{4,0},{8,4},{12,8},{16,12},{20,16},{24,20},{28,24},{0,28},{5,1},{9... | collective-permute-start | bytes 199688 | tf_op jit(solution)/shard_map/ppermute | solution.py:17
  57.2 22.1 %collective-permute-start.9 = (f32[1,256,1,130]{1,3,2,0:T(8,128)}, f32[1,256,1,130]{1,3,2,0:T(8,128)}, u32[]{:S(2)}, u32[]{:S(2)}) collective-permute-start(f32[1,256,1,130]{1,3,2,0:T(8,128)} %get-tuple-element.328), channel_id=1, source_target_pairs={{4,0},{8,4},{12,8},{16,12},{20,16},{24,20},{28,24},{5,1},{9,5},{13... | collective-permute-start | bytes 399368 | tf_op jit(solution)/shard_map/ppermute | solution.py:17
  58.5 19.9 %collective-permute-start.8 = (f32[1,256,1,130]{1,3,2,0:T(8,128)}, f32[1,256,1,130]{1,3,2,0:T(8,128)}, u32[]{:S(2)}, u32[]{:S(2)}) collective-permute-start(f32[1,256,1,130]{1,3,2,0:T(8,128)} %get-tuple-element.329), channel_id=1, source_target_pairs={{0,4},{4,8},{8,12},{12,16},{16,20},{20,24},{24,28},{1,5},{5,9},{9,... | collective-permute-start | bytes 399368 | tf_op jit(solution)/shard_map/ppermute | solution.py:15
  64.7 7.2 %collective-permute-start.2 = (bf16[1,256,1,130]{1,3,2,0:T(8,128)(2,1)}, bf16[1,256,1,130]{1,3,2,0:T(8,128)(2,1)}, u32[]{:S(2)}, u32[]{:S(2)}) collective-permute-start(bf16[1,256,1,130]{1,3,2,0:T(8,128)(2,1)} %get-tuple-element.345), channel_id=1, source_target_pairs={{0,4},{4,8},{8,12},{12,16},{16,20},{20,24},{24,28},{28,0},{1,5},{5... | collective-permute-start | bytes 199688 | tf_op jit(solution)/shard_map/ppermute | solution.py:15
  80.3 6.1 %collective-permute-start.10 = (f32[1,256,8,1]{1,3,2,0:T(1,128)S(1)}, f32[1,256,8,1]{1,3,2,0:T(1,128)S(1)}, u32[]{:S(2)}, u32[]{:S(2)}) collective-permute-start(f32[1,256,8,1]{1,3,2,0:T(1,128)S(1)} %get-tuple-element.335), channel_id=1, source_target_pairs={{0,32},{32,64},{64,96},{96,128},{128,160},{160,192},{192,224},{224... | collective-permute-start | bytes 24584 | tf_op jit(solution)/shard_map/ppermute | solution.py:15
  86.4 3.7 collective-permute-start.11
  92.5 11.4 %copy-start.11 = (bf16[1,9,256,8,128]{2,4,1,3,0:T(8,128)(2,1)S(1)}, bf16[1,9,256,8,128]{2,4,1,3,0:T(8,128)(2,1)}, u32[]{:S(2)}) copy-start(bf16[1,9,256,8,128]{2,4,1,3,0:T(8,128)(2,1)} %copy-done.10) | copy-start | bytes 14155780
  97.2 2.6 collective-permute-start.4
  97.8 3.7 collective-permute-start.5
  101.5 5.9 %collective-permute-start.7 = (bf16[1,256,1,130]{1,3,2,0:T(8,128)(2,1)S(1)}, bf16[1,256,1,130]{1,3,2,0:T(8,128)(2,1)S(1)}, u32[]{:S(2)}, u32[]{:S(2)}) collective-permute-start(bf16[1,256,1,130]{1,3,2,0:T(8,128)(2,1)S(1)} %get-tuple-element.340), channel_id=1, source_target_pairs={{4,0},{8,4},{12,8},{16,12},{20,16},{24,20},{28,24},{0,28},{5,1},{9... | collective-permute-start | bytes 199688 | tf_op jit(solution)/shard_map/ppermute | solution.py:17
  106.7 6.8 %collective-permute-start.6 = (bf16[1,256,1,130]{1,3,2,0:T(8,128)(2,1)S(1)}, bf16[1,256,1,130]{1,3,2,0:T(8,128)(2,1)S(1)}, u32[]{:S(2)}, u32[]{:S(2)}) collective-permute-start(bf16[1,256,1,130]{1,3,2,0:T(8,128)(2,1)S(1)} %get-tuple-element.341), channel_id=1, source_target_pairs={{0,4},{4,8},{8,12},{12,16},{16,20},{20,24},{24,28},{28,0},{1,5},{5... | collective-permute-start | bytes 199688 | tf_op jit(solution)/shard_map/ppermute | solution.py:15
  120.1 243.0 %all-reduce.9.cloned.1.call-start = ((), (), s32[]{:S(2)}) async-start(), calls=%async_computation.1 | async-start | bytes 9437184 | tf_op jit(solution)/shard_map/psum | solution.py:119
  300.5 7.0 %collective-permute-start.12 = (f32[1,256,1,130]{1,3,2,0:T(8,128)}, f32[1,256,1,130]{1,3,2,0:T(8,128)S(1)}, u32[]{:S(2)}, u32[]{:S(2)}) collective-permute-start(f32[1,256,1,130]{1,3,2,0:T(8,128)} %get-tuple-element.325), channel_id=1, source_target_pairs={{0,4},{4,8},{8,12},{12,16},{16,20},{20,24},{24,28},{1,5},{5,9},{9,... | collective-permute-start | bytes 399368 | tf_op jit(solution)/shard_map/ppermute | solution.py:15
  305.2 11.7 %copy-start.5 = (bf16[9,256,256]{2,1,0:T(8,128)(2,1)S(1)}, bf16[9,256,256]{2,1,0:T(8,128)(2,1)}, u32[]{:S(2)}) copy-start(bf16[9,256,256]{2,1,0:T(8,128)(2,1)} %param.59) | copy-start | bytes 3538948
  305.2 8.1 %collective-permute-start.13 = (f32[1,256,1,130]{1,3,2,0:T(8,128)S(1)}, f32[1,256,1,130]{1,3,2,0:T(8,128)S(1)}, u32[]{:S(2)}, u32[]{:S(2)}) collective-permute-start(f32[1,256,1,130]{1,3,2,0:T(8,128)S(1)} %get-tuple-element.324), channel_id=1, source_target_pairs={{4,0},{8,4},{12,8},{16,12},{20,16},{24,20},{28,24},{5,1},{9,5},{13... | collective-permute-start | bytes 399368 | tf_op jit(solution)/shard_map/ppermute | solution.py:17
  314.4 7.7 %collective-permute-start.14 = (f32[1,256,8,1]{1,3,2,0:T(1,128)S(1)}, f32[1,256,8,1]{1,3,2,0:T(1,128)S(1)}, u32[]{:S(2)}, u32[]{:S(2)}) collective-permute-start(f32[1,256,8,1]{1,3,2,0:T(1,128)S(1)} %get-tuple-element.333), channel_id=1, source_target_pairs={{0,32},{32,64},{64,96},{96,128},{128,160},{160,192},{192,224},{224... | collective-permute-start | bytes 24584 | tf_op jit(solution)/shard_map/ppermute | solution.py:15
  316.8 5.1 %copy-start.3 = (f32[1,256,8,130]{1,3,2,0:T(8,128)S(1)}, f32[1,256,8,130]{1,3,2,0:T(8,128)}, u32[]{:S(2)}) copy-start(f32[1,256,8,130]{1,3,2,0:T(8,128)} %copy-done.2) | copy-start | bytes 3194884
  322.0 4.5 %collective-permute-start.15 = (f32[1,256,8,1]{1,3,2,0:T(1,128)S(1)}, f32[1,256,8,1]{1,3,2,0:T(1,128)S(1)}, u32[]{:S(2)}, u32[]{:S(2)}) collective-permute-start(f32[1,256,8,1]{1,3,2,0:T(1,128)S(1)} %get-tuple-element.332), channel_id=1, source_target_pairs={{32,0},{64,32},{96,64},{128,96},{160,128},{192,160},{224,192},{0,2... | collective-permute-start | bytes 24584 | tf_op jit(solution)/shard_map/ppermute | solution.py:17
  (7 other events, 10.9 us)
Sparse Core Ops, SparseCore 0:
  120.2 122.2 all-reduce.6
  245.0 118.0 all-reduce.8
